TPU v7x, 256 devices: a whole 4x4x8 slice. The times are simulated.
256 devices in a mesh: replica: 32 (over y, z_lo, core), fsdp: 8 (over x, z_hi).
Axes of the slice: x: 4, y: 4, z: 8 (z_hi: 2, z_lo: 4; z = z_hi * 4 + z_lo), core: 2. Of those that a mesh axis runs over, the one named last changes fastest.
Arguments:
- tokens: bfloat16 [98304, 8192], P(('replica', 'fsdp')), may hold values from -6 to 6
- inner_weight: bfloat16 [32, 8192, 512], P('replica', 'fsdp'), may hold values from -0.0625 to 0.0625
- cotangent: bfloat16 [98304, 512], P(('replica', 'fsdp')), may hold values from -0.059814453 to 0.059814453
- local_weights: bfloat16 [32, 2, 8192, 896], P('replica', None, 'fsdp'), may hold values from -3 to 3
- anchor: bfloat16 [2, 8, 1024, 896], P(None, 'fsdp', 'replica'), may hold values from -1.5 to 1.5
- momentum: float32 [2, 8, 1024, 896], P(None, 'fsdp', 'replica'), may hold values from -1.5 to 1.5
Outputs:
- keys: bfloat16 [98304, 512], P(('replica', 'fsdp'))
- weight_grad: bfloat16 [32, 8192, 512], P('replica', 'fsdp')
- new_weights: bfloat16 [2, 8192, 896], P(None, 'fsdp')
- new_momentum: float32 [2, 8, 1024, 896], P(None, 'fsdp', 'replica')
All inputs are finite; a program needn't handle non-finite values.
Results may differ from a plain program's by a relative error of at most 0.017.
Values may be sent and summed in bfloat16 or wider, within the bound.
A program may use at most 128 MiB of HBM per device.

v0:
```python
import jax
import jax.numpy as jnp
from jax import lax
from jax.sharding import PartitionSpec as P

outer_rate = 0.7
momentum_decay = 0.9


def outer_step(local_weights, anchor, momentum):
    workers = lax.axis_size("replica")
    local_slab = local_weights[0].astype(jnp.float32)
    summed = lax.psum_scatter(local_slab, "replica", scatter_dimension=1, tiled=True)
    average = summed / workers
    anchor_now = anchor[:, 0].astype(jnp.float32)
    pseudo_grad = anchor_now - average
    momentum_new = momentum_decay * momentum[:, 0] + pseudo_grad
    new_piece = (anchor_now - outer_rate * (pseudo_grad + momentum_decay * momentum_new)).astype(
        jnp.bfloat16
    )
    gathered = lax.all_gather(new_piece, "replica", axis=1, tiled=True)
    return (gathered, momentum_new[:, None])


def inner_pass(tokens, inner_weight, cotangent):
    weight = inner_weight[0]
    columns = tokens
    key_rows = jnp.dot(
        columns,
        lax.all_gather(weight, "fsdp", axis=0, tiled=True),
        preferred_element_type=jnp.float32,
    ).astype(jnp.bfloat16)
    columns = tokens
    grad_sum = lax.psum_scatter(
        lax.dot_general(
            columns, cotangent, (((0,), (0,)), ((), ())), preferred_element_type=jnp.float32
        ).astype(jnp.bfloat16),
        "fsdp",
        scatter_dimension=0,
        tiled=True,
    )
    return (key_rows, grad_sum[None])


def shards(tokens, inner_weight, cotangent, local_weights, anchor, momentum):
    new_weights, new_momentum = outer_step(local_weights, anchor, momentum)
    keys, weight_grad = inner_pass(tokens, inner_weight, cotangent)
    return (keys, weight_grad, new_weights, new_momentum)


def solution(mesh):
    return jax.shard_map(
        shards,
        mesh=mesh,
        in_specs=(
            P(("replica", "fsdp"), None),
            P("replica", "fsdp", None),
            P(("replica", "fsdp"), None),
            P("replica", None, "fsdp", None),
            P(None, "fsdp", "replica", None),
            P(None, "fsdp", "replica", None),
        ),
        out_specs=(
            P(("replica", "fsdp"), None),
            P("replica", "fsdp", None),
            P(None, "fsdp", None),
            P(None, "fsdp", "replica", None),
        ),
        check_vma=False,
    )
```

profile of v0, /device:TPU:32, one launch (start us, length us, event | category | flops | bytes accessed | tf_op | source)
XLA Modules:
  0.0 541.9 jit_solution(11902919102617137104)
XLA Ops:
  8.0 0.0 copy-start
  8.0 0.0 reduce-scatter.5.cloned.1.call-start
  8.1 5.6 %bitcast_convert_fusion = f32[2,1024,896]{2,1,0:T(8,128)} fusion(bf16[1,2,1024,896]{3,2,1,0:T(8,128)(2,1)} %param.9), kind=kLoop, calls=%fused_computation.3 | loop fusion | flops 1835008 | bytes 11010048 | tf_op jit(solution)/shard_map/convert_element_type | solution.py:12
  13.6 0.0 copy-start.1
  13.6 0.0 copy-start.2
  13.6 0.0 reduce-scatter.5.cloned.1.call-update
  13.6 0.0 all-gather.6.cloned.1.call-start
  13.7 0.5 all-gather.6.cloned.1.call-update
  14.2 0.0 all-gather.4.cloned.1.call-start
  14.3 259.8 %reduce-scatter.5.cloned.1.call-done = f32[2,32,896]{2,1,0:T(8,128)} async-done(((f32[2,1024,896]{2,1,0:T(8,128)}), f32[2,32,896]{2,1,0:T(8,128)}) %reduce-scatter.5.cloned.1.call-update) | async-done | bytes 229392 | tf_op jit(solution)/shard_map/reduce_scatter | solution.py:13
  274.1 0.0 copy-done.1
  274.1 0.0 copy-done.2
  274.1 1.7 fusion.6
  275.8 0.0 all-gather.4.cloned.1.call-update
  275.8 0.0 reduce-scatter.3.cloned.1.call-start
  275.9 0.0 copy-done
  275.9 9.6 %convolution_convert_fusion = bf16[8192,512]{1,0:T(8,128)(2,1)} fusion(bf16[384,8192]{1,0:T(8,128)(2,1)} %param.6, bf16[384,512]{1,0:T(8,128)(2,1)S(1)} %copy-done), kind=kOutput, calls=%fused_computation | convolution fusion | flops 3225419776 | bytes 15073280 | tf_op jit(solution)/shard_map/dot_general | solution.py:35
  285.5 0.0 reduce-scatter.3.cloned.1.call-update
  285.5 0.0 all-gather.6.cloned.1.call-done
  285.6 9.4 %fusion.2 = bf16[384,512]{1,0:T(8,128)(2,1)} fusion(bf16[384,8192]{1,0:T(8,128)(2,1)} %param.6, bf16[1,8192,512]{2,1,0:T(8,128)(2,1)} %all-gather.6.cloned.1.call-done), kind=kOutput, calls=%fused_computation.4 | convolution fusion | flops 3221422080 | bytes 15073280 | tf_op jit(solution)/shard_map/dot_general | solution.py:28
  294.9 49.3 %all-gather.4.cloned.1.call-done = bf16[2,1024,896]{2,1,0:T(8,128)(2,1)} async-done(((bf16[2,32,896]{2,1,0:T(8,128)(2,1)}), bf16[2,1024,896]{2,1,0:T(8,128)(2,1)}) %all-gather.4.cloned.1.call-update) | async-done | bytes 3670032 | tf_op jit(solution)/shard_map/all_gather | solution.py:21
  344.2 185.9 %reduce-scatter.3.cloned.1.call-done = bf16[1024,512]{1,0:T(8,128)(2,1)} async-done(((bf16[8192,512]{1,0:T(8,128)(2,1)}), bf16[1024,512]{1,0:T(8,128)(2,1)}) %reduce-scatter.3.cloned.1.call-update) | async-done | bytes 1048592 | tf_op jit(solution)/shard_map/reduce_scatter | solution.py:34
  530.1 4.2 copy.13
Async XLA Ops:
  8.0 267.9 %copy-start = (bf16[384,512]{1,0:T(8,128)(2,1)S(1)}, bf16[384,512]{1,0:T(8,128)(2,1)}, u32[]{:S(2)}) copy-start(bf16[384,512]{1,0:T(8,128)(2,1)} %param.8) | copy-start | bytes 1179652
  8.0 266.0 %reduce-scatter.5.cloned.1.call-start = ((), (), s32[]{:S(2)}) async-start(), calls=%async_computation.3 | async-start | bytes 7569408 | tf_op jit(solution)/shard_map/reduce_scatter | solution.py:13
  13.6 260.4 %copy-start.1 = (f32[2,1,32,896]{3,2,1,0:T(8,128)S(1)}, f32[2,1,32,896]{3,2,1,0:T(8,128)}, u32[]{:S(2)}) copy-start(f32[2,1,32,896]{3,2,1,0:T(8,128)} %param.11) | copy-start | bytes 688132
  13.6 260.4 %copy-start.2 = (bf16[2,1,32,896]{3,2,1,0:T(8,128)(2,1)S(1)}, bf16[2,1,32,896]{3,2,1,0:T(8,128)(2,1)}, u32[]{:S(2)}) copy-start(bf16[2,1,32,896]{3,2,1,0:T(8,128)(2,1)} %param.10) | copy-start | bytes 344068
  13.6 271.9 %all-gather.6.cloned.1.call-start = ((), (), s32[]{:S(2)}) async-start(), calls=%async_computation.5 | async-start | bytes 9437184 | tf_op jit(solution)/shard_map/all_gather | solution.py:30
  14.2 330.0 %all-gather.4.cloned.1.call-start = ((), (), s32[]{:S(2)}) async-start(), calls=%async_computation.4 | async-start | bytes 3784704 | tf_op jit(solution)/shard_map/all_gather | solution.py:21
  275.8 254.3 %reduce-scatter.3.cloned.1.call-start = ((), (), s32[]{:S(2)}) async-start(), calls=%async_computation.2 | async-start | bytes 9437184 | tf_op jit(solution)/shard_map/reduce_scatter | solution.py:34
Sparse Core Ops, SparseCore 0:
  13.8 260.2 reduce-scatter.4
Sparse Core Ops, SparseCore 1:
  16.8 178.4 all-gather.5
  275.9 68.2 all-gather.3
  348.8 181.3 reduce-scatter.2
where the time goes:
time: 542 us
  waiting for transfers between devices  496 us (92%)
  matrix products  19 us (4%)
  between operations  15.7 us (3%)
  other arithmetic  7.29 us (1%)
    reduce_scatter x1, waiting for transfers between devices, outer_step(): lax.psum_scatter(local_slab, 'replica', scatter_dimension=1, tiled=True)  260 us
    reduce_scatter x1, waiting for transfers between devices, inner_pass(): lax.psum_scatter(lax.dot_general(columns, cotangent, (((0,), (0,)), ((),...  186 us
    all_gather x1, waiting for transfers between devices, outer_step(): gathered = lax.all_gather(new_piece, 'replica', axis=1, tiled=True)  49.3 us
  transfers between devices with their start and end apart: 4, of which 3 were waited for; matrix products, arithmetic and copies ran while one was open for 4% of the time, Pallas kernels for 0%

commit v1 on v0

--- a/solution.py
+++ b/solution.py
@@ -18,7 +18,9 @@
     new_piece = (anchor_now - outer_rate * (pseudo_grad + momentum_decay * momentum_new)).astype(
         jnp.bfloat16
     )
-    gathered = lax.all_gather(new_piece, "replica", axis=1, tiled=True)
+    gathered = jnp.concatenate(
+        lax.all_to_all(jnp.stack([new_piece] * lax.axis_size("replica")), "replica", 0, 0), axis=1
+    )
     return (gathered, momentum_new[:, None])
 
 

time: 542 us -> 509 us (0.939)
  waiting for transfers between devices: 496 us -> 450 us
  starting transfers between devices: 0.17 us -> 11 us
    all_to_all x0 -> x1, waiting for transfers between devices: none -> 160 us  [outer_step(): lax.all_to_all(jnp.stack([new_piece] * lax.axis_size('replica')), 'replic...]
    reduce_scatter x1, waiting for transfers between devices: 186 us -> 39.4 us  [inner_pass(): lax.psum_scatter(lax.dot_general(columns, cotangent, (((0,), (0,)), ((),...]
    all_gather x1 -> x0, waiting for transfers between devices: 49.3 us -> none  [outer_step(): gathered = lax.all_gather(new_piece, 'replica', axis=1, tiled=True)]
    all_to_all x0 -> x1, starting transfers between devices: none -> 10.9 us  [outer_step(): lax.all_to_all(jnp.stack([new_piece] * lax.axis_size('replica')), 'replic...]
    reduce_scatter x1, waiting for transfers between devices: 260 us -> 250 us  [outer_step(): lax.psum_scatter(local_slab, 'replica', scatter_dimension=1, tiled=True)]
  transfers between devices with their start and end apart: 4 -> 4, of which waited for: 3 -> 3; matrix products, arithmetic and copies ran while one was open for 4% -> 5% of each run, Pallas kernels for 0% -> 0%
where the time goes in v1:
time: 509 us
  waiting for transfers between devices  450 us (88%)
  matrix products  19 us (4%)
  between operations  15.5 us (3%)
  starting transfers between devices  11 us (2%)
  other arithmetic  7.18 us (1%)
  local copies, waits for them, and re-layouts  6.55 us (1%)
    reduce_scatter x1, waiting for transfers between devices, outer_step(): lax.psum_scatter(local_slab, 'replica', scatter_dimension=1, tiled=True)  250 us
    all_to_all x1, waiting for transfers between devices, outer_step(): lax.all_to_all(jnp.stack([new_piece] * lax.axis_size('replica')), 'replic...  160 us
    reduce_scatter x1, waiting for transfers between devices, inner_pass(): lax.psum_scatter(lax.dot_general(columns, cotangent, (((0,), (0,)), ((),...  39.4 us
    all_to_all x1, starting transfers between devices, outer_step(): lax.all_to_all(jnp.stack([new_piece] * lax.axis_size('replica')), 'replic...  10.9 us
  transfers between devices with their start and end apart: 4, of which 3 were waited for; matrix products, arithmetic and copies ran while one was open for 5% of the time, Pallas kernels for 0%

profile of v1, /device:TPU:32, one launch (start us, length us, event | category | flops | bytes accessed | tf_op | source)
XLA Modules:
  0.0 509.0 jit_solution(8265906867997058483)
XLA Ops:
  8.0 0.0 copy-start
  8.0 0.0 reduce-scatter.5.cloned.1.call-start
  8.1 5.5 %bitcast_convert_fusion = f32[2,1024,896]{2,1,0:T(8,128)} fusion(bf16[1,2,1024,896]{3,2,1,0:T(8,128)(2,1)} %param.9), kind=kLoop, calls=%fused_computation.3 | loop fusion | flops 1835008 | bytes 11010048 | tf_op jit(solution)/shard_map/convert_element_type | solution.py:12
  13.5 0.0 reduce-scatter.5.cloned.1.call-update
  13.6 0.0 all-gather.3.cloned.1.call-start
  13.6 0.5 all-gather.3.cloned.1.call-update
  14.1 0.0 reduce-scatter.3.cloned.1.call-start
  14.2 0.0 copy-done
  14.2 9.6 %convolution_convert_fusion = bf16[8192,512]{1,0:T(8,128)(2,1)} fusion(bf16[384,8192]{1,0:T(8,128)(2,1)} %param.6, bf16[384,512]{1,0:T(8,128)(2,1)S(1)} %copy-done), kind=kOutput, calls=%fused_computation | convolution fusion | flops 3225419776 | bytes 15073280 | tf_op jit(solution)/shard_map/dot_general | solution.py:37
  23.8 0.0 copy-start.1
  23.8 0.0 copy-start.2
  23.8 0.0 reduce-scatter.3.cloned.1.call-update
  23.9 250.1 %reduce-scatter.5.cloned.1.call-done = f32[2,32,896]{2,1,0:T(8,128)} async-done(((f32[2,1024,896]{2,1,0:T(8,128)}), f32[2,32,896]{2,1,0:T(8,128)}) %reduce-scatter.5.cloned.1.call-update) | async-done | bytes 229392 | tf_op jit(solution)/shard_map/reduce_scatter | solution.py:13
  274.0 0.0 copy-done.1
  274.0 0.0 copy-done.2
  274.0 1.7 fusion.6
  275.7 2.3 stack.2
  278.0 10.9 %all-to-all-start = ((bf16[32,2,32,896]{3,2,1,0:T(8,128)(2,1)}), bf16[32,2,32,896]{3,2,1,0:T(8,128)(2,1)}, u32[]{:S(2)}, u32[]{:S(2)}) async-start(bf16[32,2,32,896]{3,2,1,0:T(8,128)(2,1)} %stack.2), calls=%async_computation.2 | async-start | bytes 7340032 | tf_op jit(solution)/shard_map/all_to_all | solution.py:22
  288.9 0.0 all-gather.3.cloned.1.call-done
  288.9 9.4 %fusion.2 = bf16[384,512]{1,0:T(8,128)(2,1)} fusion(bf16[384,8192]{1,0:T(8,128)(2,1)} %param.6, bf16[1,8192,512]{2,1,0:T(8,128)(2,1)} %all-gather.3.cloned.1.call-done), kind=kOutput, calls=%fused_computation.4 | convolution fusion | flops 3221422080 | bytes 15073280 | tf_op jit(solution)/shard_map/dot_general | solution.py:30
  298.3 159.7 %all-to-all-done = bf16[32,2,32,896]{3,2,1,0:T(8,128)(2,1)} async-done(((bf16[32,2,32,896]{3,2,1,0:T(8,128)(2,1)}), bf16[32,2,32,896]{3,2,1,0:T(8,128)(2,1)}, u32[]{:S(2)}, u32[]{:S(2)}) %all-to-all-start) | async-done | bytes 3670048 | tf_op jit(solution)/shard_map/all_to_all | solution.py:22
  458.0 4.2 copy.16
  462.2 39.4 %reduce-scatter.3.cloned.1.call-done = bf16[1024,512]{1,0:T(8,128)(2,1)} async-done(((bf16[8192,512]{1,0:T(8,128)(2,1)}), bf16[1024,512]{1,0:T(8,128)(2,1)}) %reduce-scatter.3.cloned.1.call-update) | async-done | bytes 1048592 | tf_op jit(solution)/shard_map/reduce_scatter | solution.py:36
Async XLA Ops:
  8.0 6.2 %copy-start = (bf16[384,512]{1,0:T(8,128)(2,1)S(1)}, bf16[384,512]{1,0:T(8,128)(2,1)}, u32[]{:S(2)}) copy-start(bf16[384,512]{1,0:T(8,128)(2,1)} %param.8) | copy-start | bytes 1179652
  8.0 266.0 %reduce-scatter.5.cloned.1.call-start = ((), (), s32[]{:S(2)}) async-start(), calls=%async_computation.4 | async-start | bytes 7569408 | tf_op jit(solution)/shard_map/reduce_scatter | solution.py:13
  13.6 275.3 %all-gather.3.cloned.1.call-start = ((), (), s32[]{:S(2)}) async-start(), calls=%async_computation.5 | async-start | bytes 9437184 | tf_op jit(solution)/shard_map/all_gather | solution.py:32
  14.1 487.4 %reduce-scatter.3.cloned.1.call-start = ((), (), s32[]{:S(2)}) async-start(), calls=%async_computation.3 | async-start | bytes 9437184 | tf_op jit(solution)/shard_map/reduce_scatter | solution.py:36
  23.8 250.1 %copy-start.1 = (f32[2,1,32,896]{3,2,1,0:T(8,128)S(1)}, f32[2,1,32,896]{3,2,1,0:T(8,128)}, u32[]{:S(2)}) copy-start(f32[2,1,32,896]{3,2,1,0:T(8,128)} %param.11) | copy-start | bytes 688132
  23.8 250.1 %copy-start.2 = (bf16[2,1,32,896]{3,2,1,0:T(8,128)(2,1)S(1)}, bf16[2,1,32,896]{3,2,1,0:T(8,128)(2,1)}, u32[]{:S(2)}) copy-start(bf16[2,1,32,896]{3,2,1,0:T(8,128)(2,1)} %param.10) | copy-start | bytes 344068
  278.0 180.0 %all-to-all-start = ((bf16[32,2,32,896]{3,2,1,0:T(8,128)(2,1)}), bf16[32,2,32,896]{3,2,1,0:T(8,128)(2,1)}, u32[]{:S(2)}, u32[]{:S(2)}) async-start(bf16[32,2,32,896]{3,2,1,0:T(8,128)(2,1)} %stack.2), calls=%async_computation.2 | async-start | bytes 7340032 | tf_op jit(solution)/shard_map/all_to_all | solution.py:22
Sparse Core Ops, SparseCore 0:
  13.7 260.2 reduce-scatter.4
  278.7 222.8 reduce-scatter.2
Sparse Core Ops, SparseCore 1:
  16.7 178.4 all-gather.2
